TPU v7x, 32 devices: a whole 2x2x4 slice. The times are simulated.
32 devices in a mesh: brow: 4 (over z), bcol: 8 (over y, x, core).
Axes of the slice: x: 2, y: 2, z: 4, core: 2. Of those that a mesh axis runs over, the one named last changes fastest.
Arguments:
- anc_tiles: int32 [1, 12], replicated, may hold values from 0 to 31, as said below
- ancestor_inverse: float32 [16384, 16384], P('brow', 'bcol'), as said below
- factor_pieces: float32 [16384, 1536], P('bcol', 'brow'), may hold values from -6 to 6
Outputs:
- inverse_rows: float32 [1536, 16384], P('bcol', 'brow')
Inputs may be any that keep to these rules, and one draw needn't show every extreme that they name: `anc_tiles`: each row lists 12 different tiles; tile 32 - 1 is listed in every row, tile 0 in row 0. ancestor_inverse is symmetric.
All inputs are finite; a program needn't handle non-finite values.
Results may differ from a plain program's by a relative error of at most 0.00007.
Values sent between devices are 32-bit elements; how exact they have to be, the bound alone decides.
A program may use at most 128 MiB of HBM per device.

v0:
```python
import jax
import jax.numpy as jnp
from jax import lax
from jax.sharding import PartitionSpec as P

TS = 512
W = 1536
A = 32
K = 1


def local(anc_tiles, ancestor_inverse, factor_pieces):
    col_index = lax.axis_index("bcol")
    row_index = lax.axis_index("brow")
    n_col = lax.axis_size("bcol")
    tile_ids = jnp.arange(A, dtype=jnp.int32)
    listed = jnp.sum((anc_tiles[:, :, None] == tile_ids[None, None, :]).astype(jnp.int32), axis=1)
    listed_float = (listed > 0).astype(jnp.float32)
    gathered = lax.all_gather(factor_pieces, "brow", axis=1, tiled=True)
    tiles_here = gathered.shape[0] // TS
    total_cols = gathered.shape[1]
    listed_local = lax.dynamic_slice_in_dim(listed_float, col_index * tiles_here, tiles_here, 1)
    masked = gathered.reshape(tiles_here, TS, K, W) * listed_local.T[:, None, :, None]
    masked = masked.reshape(tiles_here * TS, total_cols)
    block_rows = ancestor_inverse.shape[0]
    super_ids = jnp.arange(K, dtype=jnp.int32)
    out_rows = total_cols // n_col
    summed = lax.psum_scatter(
        lax.dot_general(
            masked,
            ancestor_inverse,
            (((0,), (1,)), ((), ())),
            precision=lax.Precision.HIGHEST,
            preferred_element_type=jnp.float32,
        ),
        "bcol",
        scatter_dimension=0,
        tiled=True,
    )
    super_of_row = (col_index * out_rows + jnp.arange(out_rows, dtype=jnp.int32)) // W
    tile_of_col = (row_index * block_rows + jnp.arange(block_rows, dtype=jnp.int32)) // TS
    onehot_super = (super_of_row[:, None] == super_ids[None, :]).astype(jnp.float32)
    onehot_tile = (tile_of_col[:, None] == tile_ids[None, :]).astype(jnp.float32)
    per_row = jnp.dot(onehot_super, listed_float, preferred_element_type=jnp.float32)
    out_mask = jnp.dot(per_row, onehot_tile.T, preferred_element_type=jnp.float32)
    return -summed * out_mask


def solution(mesh):
    in_specs = (P(), P("brow", "bcol"), P("bcol", "brow"))
    out_specs = P("bcol", "brow")
    return jax.shard_map(local, mesh=mesh, in_specs=in_specs, out_specs=out_specs, check_vma=False)
```

profile of v0, /device:TPU:0, one launch (start us, length us, event | category | flops | bytes accessed | tf_op | source)
XLA Modules:
  0.0 720.1 jit_solution(13993428021869815170)
XLA Ops:
  6.5 0.0 all-gather.2.cloned.1.call-start
  6.5 0.7 all-gather.2.cloned.1.call-update
  7.3 0.0 reduce-scatter.2.cloned.1.call-start
  7.3 0.7 fusion.10
  8.1 0.1 dynamic-slice.3
  8.1 0.1 broadcast_bitcast_fusion
  8.2 221.6 %all-gather.2.cloned.1.call-done = f32[2048,1536]{1,0:T(8,128)} async-done(((f32[2048,384]{1,0:T(8,128)}), f32[2048,1536]{1,0:T(8,128)}) %all-gather.2.cloned.1.call-update) | async-done | bytes 12582928 | tf_op jit(solution)/shard_map/all_gather | solution.py:19
  229.9 323.9 %fusion = f32[1536,4096]{1,0:T(8,128)} fusion(f32[4096,2048]{1,0:T(8,128)} %param.4, f32[2048,1536]{1,0:T(8,128)} %all-gather.2.cloned.1.call-done, f32[2048]{0:T(1024)S(1)} %bitcast.6), kind=kOutput, calls=%fused_computation | convolution fusion | flops 154621968384 | bytes 71311360 | tf_op jit(solution)/shard_map/dot_general | solution.py:29
  553.8 0.0 reduce-scatter.2.cloned.1.call-update
  553.9 155.2 %reduce-scatter.2.cloned.1.call-done = f32[192,4096]{1,0:T(8,128)} async-done(((f32[1536,4096]{1,0:T(8,128)}), f32[192,4096]{1,0:T(8,128)}) %reduce-scatter.2.cloned.1.call-update) | async-done | bytes 3145744 | tf_op jit(solution)/shard_map/reduce_scatter | solution.py:28
  709.1 4.2 convolution_multiply_fusion
  (4 shorter events, 0.0 us)
Async XLA Ops:
  6.5 223.3 %all-gather.2.cloned.1.call-start = ((), (), s32[]{:S(2)}) async-start(), calls=%async_computation.1 | async-start | bytes 15728640 | tf_op jit(solution)/shard_map/all_gather | solution.py:19
  7.3 701.8 %reduce-scatter.2.cloned.1.call-start = ((), (), s32[]{:S(2)}) async-start(), calls=%async_computation.2 | async-start | bytes 28311552 | tf_op jit(solution)/shard_map/reduce_scatter | solution.py:28
Sparse Core Ops, SparseCore 0:
  8.9 220.8 all-gather.1
  553.9 155.0 reduce-scatter.1
where the time goes:
time: 720 us
  waiting for transfers between devices  378 us (52%)
  matrix products  328 us (46%)
  between operations  13.4 us (2%)
    dot_general x1, matrix products, local(): lax.dot_general(masked, ancestor_inverse, (((0,), (1,)), ((), ())), preci...  324 us
    all_gather x1, waiting for transfers between devices, local(): gathered = lax.all_gather(factor_pieces, 'brow', axis=1, tiled=True)  222 us
    reduce_scatter x1, waiting for transfers between devices, local(): lax.psum_scatter(lax.dot_general(masked, ancestor_inverse, (((0,), (1,)),...  155 us
  transfers between devices with their start and end apart: 2, of which 2 were waited for; matrix products, arithmetic and copies ran while one was open for 0% of the time, Pallas kernels for 0%

commit v1 on v0

v1 whole, which is shorter than its diff:
```python
import jax
import jax.numpy as jnp
from jax import lax
from jax.sharding import PartitionSpec as P

TS = 512
W = 1536
A = 32
K = 1
CHUNKS = 4


def split(x):
    high = lax.reduce_precision(x, exponent_bits=8, mantissa_bits=7)
    return high.astype(jnp.bfloat16), (x - high).astype(jnp.bfloat16)


def product(x, y, **kwargs):
    return lax.dot_general(
        x, y, (((1,), (1,)), ((), ())), preferred_element_type=jnp.float32, **kwargs
    )


def local(anc_tiles, ancestor_inverse, factor_pieces):
    col_index = lax.axis_index("bcol")
    row_index = lax.axis_index("brow")
    n_col = lax.axis_size("bcol")
    n_row = lax.axis_size("brow")
    block_rows, block_cols = ancestor_inverse.shape
    tiles_col, tiles_row = block_cols // TS, block_rows // TS
    total_cols = factor_pieces.shape[1] * n_row
    tile_ids = jnp.arange(A, dtype=jnp.int32)
    listed = jnp.any(anc_tiles[:, :, None] == tile_ids[None, None, :], axis=1)

    col_super = (row_index * factor_pieces.shape[1] + jnp.arange(factor_pieces.shape[1])) // W
    listed_col = lax.dynamic_slice_in_dim(listed, col_index * tiles_col, tiles_col, 1)
    col_mask = jnp.repeat(listed_col[col_super], TS, axis=1)
    factor = jnp.where(col_mask, factor_pieces.T, 0.0)
    width = total_cols // n_col // CHUNKS
    factor = factor.reshape(-1, CHUNKS, width, block_cols)
    gathered = [
        lax.all_gather(factor[:, q], "brow", axis=0, tiled=True).reshape(-1, block_cols)
        for q in range(CHUNKS)
    ]

    sums = []
    for q in range(CHUNKS):
        part = product(gathered[q], ancestor_inverse, precision=lax.Precision.HIGH)
        sums.append(lax.psum_scatter(part, "bcol", scatter_dimension=0, tiled=True))
    summed = jnp.concatenate(sums, axis=0)

    out_rows = summed.shape[0]
    row_super = (col_index * out_rows + jnp.arange(out_rows)) // W
    listed_row = lax.dynamic_slice_in_dim(listed, row_index * tiles_row, tiles_row, 1)
    out_mask = jnp.repeat(listed_row[row_super], TS, axis=1)
    return jnp.where(out_mask, -summed, 0.0)


def solution(mesh):
    in_specs = (P(), P("brow", "bcol"), P("bcol", "brow"))
    out_specs = P("bcol", "brow")
    return jax.shard_map(local, mesh=mesh, in_specs=in_specs, out_specs=out_specs, check_vma=False)
```

time: 720 us -> 543 us (0.75)
  matrix products: 328 us -> 105 us
  waiting for transfers between devices: 378 us -> 411 us
    dot_general x2 -> x4, matrix products: 328 us -> 105 us  [product(): lax.dot_general(x, y, (((1,), (1,)), ((), ())), preferred_element_type=jn...]
    reduce_scatter x1 -> x4, waiting for transfers between devices: 155 us -> 233 us  [local(): sums.append(lax.psum_scatter(part, 'bcol', scatter_dimension=0, tiled=True))]
    all_gather x1 -> x4, waiting for transfers between devices: 222 us -> 176 us  [local(): lax.all_gather(factor[:, q], 'brow', axis=0, tiled=True)]
  transfers between devices with their start and end apart: 2 -> 8, of which waited for: 2 -> 8; matrix products, arithmetic and copies ran while one was open for 0% -> 19% of each run, Pallas kernels for 0% -> 0%
where the time goes in v1:
time: 543 us
  waiting for transfers between devices  411 us (76%)
  matrix products  105 us (19%)
  between operations  13.5 us (2%)
  local copies, waits for them, and re-layouts  6.92 us (1%)
  other arithmetic  6.4 us (1%)
    reduce_scatter x4, waiting for transfers between devices, local(): sums.append(lax.psum_scatter(part, 'bcol', scatter_dimension=0, tiled=True))  233 us
    all_gather x4, waiting for transfers between devices, local(): lax.all_gather(factor[:, q], 'brow', axis=0, tiled=True)  176 us
    dot_general x4, matrix products, product(): lax.dot_general(x, y, (((1,), (1,)), ((), ())), preferred_element_type=jn...  105 us
  transfers between devices with their start and end apart: 8, of which 8 were waited for; matrix products, arithmetic and copies ran while one was open for 19% of the time, Pallas kernels for 0%

profile of v1, /device:TPU:0, one launch (start us, length us, event | category | flops | bytes accessed | tf_op | source)
XLA Modules:
  0.0 543.0 jit_solution(9109065422733536276)
XLA Ops:
  6.5 0.0 all-gather.15.cloned.1.call-start
  6.5 0.7 fusion.1
  7.3 0.1 dynamic-slice.7
  7.4 0.5 broadcast_in_dim.19
  7.8 1.3 copy.8
  9.2 2.4 copy.6
  11.6 1.6 bitcast_select_fusion
  13.2 1.8 fusion.2
  15.0 0.0 all-gather.15.cloned.1.call-update
  15.0 0.0 all-gather.9.cloned.1.call-start
  15.0 0.7 all-gather.9.cloned.1.call-update
  15.7 0.0 all-gather.11.cloned.1.call-start
  15.8 0.7 all-gather.11.cloned.1.call-update
  16.5 0.0 all-gather.13.cloned.1.call-start
  16.5 0.5 all-gather.13.cloned.1.call-update
  17.1 0.0 reduce-scatter.11.cloned.1.call-start
  17.1 64.2 %all-gather.15.cloned.1.call-done = f32[8,1,48,2048]{3,2,1,0:T(8,128)} async-done(((f32[2,1,48,2048]{3,2,1,0:T(8,128)}), f32[8,1,48,2048]{3,2,1,0:T(8,128)}) %all-gather.15.cloned.1.call-update) | async-done | bytes 3145744 | tf_op jit(solution)/shard_map/all_gather | solution.py:42
  81.4 26.1 %fusion.6 = f32[384,4096]{1,0:T(8,128)} fusion(f32[384,2048]{1,0:T(8,128)} %bitcast.24, f32[4096,2048]{1,0:T(8,128)} %param.4), kind=kOutput, calls=%fused_computation.9 | convolution fusion | flops 19327352832 | bytes 42991616 | tf_op jit(solution)/shard_map/dot_general | solution.py:19
  107.5 0.0 reduce-scatter.11.cloned.1.call-update
  107.5 0.2 reduce-scatter.5.cloned.1.call-start
  107.7 37.4 %all-gather.9.cloned.1.call-done = f32[8,1,48,2048]{3,2,1,0:T(8,128)} async-done(((f32[2,1,48,2048]{3,2,1,0:T(8,128)}), f32[8,1,48,2048]{3,2,1,0:T(8,128)}) %all-gather.9.cloned.1.call-update) | async-done | bytes 3145744 | tf_op jit(solution)/shard_map/all_gather | solution.py:42
  145.1 26.1 %fusion.3 = f32[384,4096]{1,0:T(8,128)} fusion(f32[384,2048]{1,0:T(8,128)} %bitcast.23, f32[4096,2048]{1,0:T(8,128)} %param.4), kind=kOutput, calls=%fused_computation.6 | convolution fusion | flops 19327352832 | bytes 42991616 | tf_op jit(solution)/shard_map/dot_general | solution.py:19
  171.2 0.0 reduce-scatter.5.cloned.1.call-update
  171.3 0.0 reduce-scatter.7.cloned.1.call-start
  171.3 37.5 %all-gather.11.cloned.1.call-done = f32[8,1,48,2048]{3,2,1,0:T(8,128)} async-done(((f32[2,1,48,2048]{3,2,1,0:T(8,128)}), f32[8,1,48,2048]{3,2,1,0:T(8,128)}) %all-gather.11.cloned.1.call-update) | async-done | bytes 3145744 | tf_op jit(solution)/shard_map/all_gather | solution.py:42
  208.9 26.1 %fusion.4 = f32[384,4096]{1,0:T(8,128)} fusion(f32[384,2048]{1,0:T(8,128)} %bitcast.22, f32[4096,2048]{1,0:T(8,128)} %param.4), kind=kOutput, calls=%fused_computation.7 | convolution fusion | flops 19327352832 | bytes 42991616 | tf_op jit(solution)/shard_map/dot_general | solution.py:19
  235.0 0.0 reduce-scatter.7.cloned.1.call-update
  235.0 0.3 reduce-scatter.9.cloned.1.call-start
  235.3 37.2 %all-gather.13.cloned.1.call-done = f32[8,1,48,2048]{3,2,1,0:T(8,128)} async-done(((f32[2,1,48,2048]{3,2,1,0:T(8,128)}), f32[8,1,48,2048]{3,2,1,0:T(8,128)}) %all-gather.13.cloned.1.call-update) | async-done | bytes 3145744 | tf_op jit(solution)/shard_map/all_gather | solution.py:42
  272.5 26.1 %fusion.5 = f32[384,4096]{1,0:T(8,128)} fusion(f32[384,2048]{1,0:T(8,128)} %bitcast.21, f32[4096,2048]{1,0:T(8,128)} %param.4), kind=kOutput, calls=%fused_computation.8 | convolution fusion | flops 19327352832 | bytes 42991616 | tf_op jit(solution)/shard_map/dot_general | solution.py:19
  298.6 0.0 reduce-scatter.9.cloned.1.call-update
  298.6 0.1 dynamic-slice.6
  298.7 0.3 broadcast_in_dim.18
  299.0 0.5 copy.7
  299.5 36.6 %reduce-scatter.11.cloned.1.call-done = f32[48,4096]{1,0:T(8,128)} async-done(((f32[384,4096]{1,0:T(8,128)}), f32[48,4096]{1,0:T(8,128)}) %reduce-scatter.11.cloned.1.call-update) | async-done | bytes 786448 | tf_op jit(solution)/shard_map/reduce_scatter | solution.py:49
  336.1 65.4 %reduce-scatter.5.cloned.1.call-done = f32[48,4096]{1,0:T(8,128)} async-done(((f32[384,4096]{1,0:T(8,128)}), f32[48,4096]{1,0:T(8,128)}) %reduce-scatter.5.cloned.1.call-update) | async-done | bytes 786448 | tf_op jit(solution)/shard_map/reduce_scatter | solution.py:49
  401.5 65.2 %reduce-scatter.7.cloned.1.call-done = f32[48,4096]{1,0:T(8,128)} async-done(((f32[384,4096]{1,0:T(8,128)}), f32[48,4096]{1,0:T(8,128)}) %reduce-scatter.7.cloned.1.call-update) | async-done | bytes 786448 | tf_op jit(solution)/shard_map/reduce_scatter | solution.py:49
  466.7 65.5 %reduce-scatter.9.cloned.1.call-done = f32[48,4096]{1,0:T(8,128)} async-done(((f32[384,4096]{1,0:T(8,128)}), f32[48,4096]{1,0:T(8,128)}) %reduce-scatter.9.cloned.1.call-update) | async-done | bytes 786448 | tf_op jit(solution)/shard_map/reduce_scatter | solution.py:49
  532.2 4.0 fusion
Async XLA Ops:
  6.5 74.8 %all-gather.15.cloned.1.call-start = ((), (), s32[]{:S(2)}) async-start(), calls=%async_computation.11 | async-start | bytes 3932160 | tf_op jit(solution)/shard_map/all_gather | solution.py:42
  15.0 130.1 %all-gather.9.cloned.1.call-start = ((), (), s32[]{:S(2)}) async-start(), calls=%async_computation.8 | async-start | bytes 3932160 | tf_op jit(solution)/shard_map/all_gather | solution.py:42
  15.7 193.1 %all-gather.11.cloned.1.call-start = ((), (), s32[]{:S(2)}) async-start(), calls=%async_computation.9 | async-start | bytes 3932160 | tf_op jit(solution)/shard_map/all_gather | solution.py:42
  16.5 256.0 %all-gather.13.cloned.1.call-start = ((), (), s32[]{:S(2)}) async-start(), calls=%async_computation.10 | async-start | bytes 3932160 | tf_op jit(solution)/shard_map/all_gather | solution.py:42
  17.1 319.1 %reduce-scatter.11.cloned.1.call-start = ((), (), s32[]{:S(2)}) async-start(), calls=%async_computation.7 | async-start | bytes 7077888 | tf_op jit(solution)/shard_map/reduce_scatter | solution.py:49
  107.5 294.0 %reduce-scatter.5.cloned.1.call-start = ((), (), s32[]{:S(2)}) async-start(), calls=%async_computation.4 | async-start | bytes 7077888 | tf_op jit(solution)/shard_map/reduce_scatter | solution.py:49
  171.3 295.4 %reduce-scatter.7.cloned.1.call-start = ((), (), s32[]{:S(2)}) async-start(), calls=%async_computation.5 | async-start | bytes 7077888 | tf_op jit(solution)/shard_map/reduce_scatter | solution.py:49
  235.0 297.2 %reduce-scatter.9.cloned.1.call-start = ((), (), s32[]{:S(2)}) async-start(), calls=%async_computation.6 | async-start | bytes 7077888 | tf_op jit(solution)/shard_map/reduce_scatter | solution.py:49
Sparse Core Ops, SparseCore 0:
  15.1 66.1 all-gather.14
  82.9 62.1 all-gather.8
  146.7 62.1 all-gather.10
  210.3 62.1 all-gather.12
  275.7 60.3 reduce-scatter.10
  339.7 61.7 reduce-scatter.4
  404.9 61.7 reduce-scatter.6
  470.4 61.7 reduce-scatter.8

commit v2 on v1

--- a/solution.py
+++ b/solution.py
@@ -7,7 +7,7 @@
 W = 1536
 A = 32
 K = 1
-CHUNKS = 4
+CHUNKS = 3
 
 
 def split(x):
@@ -19,6 +19,25 @@
     return lax.dot_general(
         x, y, (((1,), (1,)), ((), ())), preferred_element_type=jnp.float32, **kwargs
     )
+
+
+def line_gather(own, following, before, row_index, n_row):
+    from_below, from_above = [], []
+    below = above = own
+    upward = [(r, r + 1) for r in range(n_row - 1)]
+    downward = [(r + 1, r) for r in range(n_row - 1)]
+    for step in range(n_row - 1):
+        if step == n_row - 2 and following is not None:
+            below, above, following = lax.optimization_barrier((below, above, following))
+        if step == 1 and before is not None:
+            below, above, before = lax.optimization_barrier((below, above, before))
+        below = lax.ppermute(below, "brow", upward)
+        above = lax.ppermute(above, "brow", downward)
+        from_below.insert(0, below)
+        from_above.append(above)
+    window = jnp.stack(from_below + [own] + from_above)
+    window = lax.dynamic_slice_in_dim(window, n_row - 1 - row_index, n_row, 0)
+    return window.reshape(-1, own.shape[-1]), following, before
 
 
 def local(anc_tiles, ancestor_inverse, factor_pieces):
@@ -38,15 +57,18 @@
     factor = jnp.where(col_mask, factor_pieces.T, 0.0)
     width = total_cols // n_col // CHUNKS
     factor = factor.reshape(-1, CHUNKS, width, block_cols)
-    gathered = [
-        lax.all_gather(factor[:, q], "brow", axis=0, tiled=True).reshape(-1, block_cols)
-        for q in range(CHUNKS)
-    ]
-
-    sums = []
+    own = [factor[:, q] for q in range(CHUNKS)]
+    parts = []
     for q in range(CHUNKS):
-        part = product(gathered[q], ancestor_inverse, precision=lax.Precision.HIGH)
-        sums.append(lax.psum_scatter(part, "bcol", scatter_dimension=0, tiled=True))
+        following = own[q + 1] if q + 1 < CHUNKS else None
+        before = parts[q - 1] if q > 0 else None
+        whole, following, before = line_gather(own[q], following, before, row_index, n_row)
+        if q > 0:
+            parts[q - 1] = before
+        if q + 1 < CHUNKS:
+            own[q + 1] = following
+        parts.append(product(whole, ancestor_inverse, precision=lax.Precision.HIGH))
+    sums = [lax.psum_scatter(part, "bcol", scatter_dimension=0, tiled=True) for part in parts]
     summed = jnp.concatenate(sums, axis=0)
 
     out_rows = summed.shape[0]

time: 543 us -> 426 us (0.78)
  waiting for transfers between devices: 411 us -> 235 us
  starting transfers between devices: 0.68 us -> 52.5 us
  local copies, waits for them, and re-layouts: 6.92 us -> 19.9 us
  matrix products: 105 us -> 96.6 us
    all_gather x4 -> x0, waiting for transfers between devices: 176 us -> none  [local(): lax.all_gather(factor[:, q], 'brow', axis=0, tiled=True)]
    ppermute x0 -> x18, waiting for transfers between devices: none -> 166 us  [the longest x9 85.2 us: line_gather(): above = lax.ppermute(above, 'brow', downward)]
    reduce_scatter x4 -> x3, waiting for transfers between devices: 233 us -> 68.8 us  [local(): lax.psum_scatter(part, 'bcol', scatter_dimension=0, tiled=True)]
    ppermute x0 -> x18, starting transfers between devices: none -> 52.4 us  [the longest x9 40.3 us: line_gather(): below = lax.ppermute(below, 'brow', upward)]
    unnamed x3 -> x35, local copies, waits for them, and re-layouts: 4.23 us -> 16.4 us
    dot_general x4 -> x3, matrix products: 105 us -> 96.6 us  [product(): lax.dot_general(x, y, (((1,), (1,)), ((), ())), preferred_element_type=jn...]
  transfers between devices with their start and end apart: 8 -> 21, of which waited for: 8 -> 13; matrix products, arithmetic and copies ran while one was open for 19% -> 25% of each run, Pallas kernels for 0% -> 0%
where the time goes in v2:
time: 426 us; the launch traced here: 425 us
  waiting for transfers between devices  235 us (55%)
  matrix products  96.6 us (23%)
  starting transfers between devices  52.5 us (12%)
  local copies, waits for them, and re-layouts  19.9 us (5%)
  between operations  13.5 us (3%)
  other arithmetic  7.36 us (2%)
    dot_general x3, matrix products, product(): lax.dot_general(x, y, (((1,), (1,)), ((), ())), preferred_element_type=jn...  96.6 us
    ppermute x9, waiting for transfers between devices, line_gather(): above = lax.ppermute(above, 'brow', downward)  85.2 us
    ppermute x9, waiting for transfers between devices, line_gather(): below = lax.ppermute(below, 'brow', upward)  81 us
    reduce_scatter x3, waiting for transfers between devices, local(): lax.psum_scatter(part, 'bcol', scatter_dimension=0, tiled=True)  68.8 us
    ppermute x9, starting transfers between devices, line_gather(): below = lax.ppermute(below, 'brow', upward)  40.3 us
    unnamed x35, local copies, waits for them, and re-layouts  16.4 us
    ppermute x9, starting transfers between devices, line_gather(): above = lax.ppermute(above, 'brow', downward)  12.1 us
  transfers between devices with their start and end apart: 21, of which 13 were waited for; matrix products, arithmetic and copies ran while one was open for 25% of the time, Pallas kernels for 0%

profile of v2, /device:TPU:0, one launch (start us, length us, event | category | flops | bytes accessed | tf_op | source)
XLA Modules:
  0.0 424.9 jit_solution(9237053874122433239)
XLA Ops:
  6.5 0.7 fusion.1
  7.8 1.3 copy.7
  9.2 3.5 copy.5
  12.7 2.6 bitcast_select_fusion
  15.3 1.6 slice_bitcast_fusion
  16.9 1.3 collective-permute-start.2
  18.2 5.6 %collective-permute-start = (f32[2,64,2048]{2,1,0:T(8,128)S(1)}, f32[2,64,2048]{2,1,0:T(8,128)S(1)}, u32[]{:S(2)}, u32[]{:S(2)}) collective-permute-start(f32[2,64,2048]{2,1,0:T(8,128)S(1)} %get-tuple-element.31), channel_id=1, source_target_pairs={{0,8},{8,16},{16,24},{1,9},{9,17},{17,25},{2,10},{10,18},{18,26},{... | collective-permute-start | bytes 3145736 | tf_op jit(solution)/shard_map/ppermute | solution.py:34
  23.8 21.2 %collective-permute-done.2 = f32[2,64,2048]{2,1,0:T(8,128)S(1)} collective-permute-done((f32[2,64,2048]{2,1,0:T(8,128)S(1)}, f32[2,64,2048]{2,1,0:T(8,128)S(1)}, u32[]{:S(2)}, u32[]{:S(2)}) %collective-permute-start.2) | collective-permute-done | bytes 1048608 | tf_op jit(solution)/shard_map/ppermute | solution.py:35
  45.0 1.0 copy-done.2
  46.0 1.3 collective-permute-start.3
  47.3 5.5 %collective-permute-start.1 = (f32[2,64,2048]{2,1,0:T(8,128)S(1)}, f32[2,64,2048]{2,1,0:T(8,128)}, u32[]{:S(2)}, u32[]{:S(2)}) collective-permute-start(f32[2,64,2048]{2,1,0:T(8,128)S(1)} %collective-permute-done), channel_id=1, source_target_pairs={{0,8},{8,16},{16,24},{1,9},{9,17},{17,25},{2,10},{10,18},{18,26},{... | collective-permute-start | bytes 3145736 | tf_op jit(solution)/shard_map/ppermute | solution.py:34
  52.8 19.4 %collective-permute-done.3 = f32[2,64,2048]{2,1,0:T(8,128)S(1)} collective-permute-done((f32[2,64,2048]{2,1,0:T(8,128)S(1)}, f32[2,64,2048]{2,1,0:T(8,128)S(1)}, u32[]{:S(2)}, u32[]{:S(2)}) %collective-permute-start.3) | collective-permute-done | bytes 1048608 | tf_op jit(solution)/shard_map/ppermute | solution.py:35
  72.2 1.0 copy-done.4
  73.4 5.5 %collective-permute-start.6 = (f32[2,64,2048]{2,1,0:T(8,128)}, f32[2,64,2048]{2,1,0:T(8,128)}, u32[]{:S(2)}, u32[]{:S(2)}) collective-permute-start(f32[2,64,2048]{2,1,0:T(8,128)} %collective-permute-done.1), channel_id=1, source_target_pairs={{0,8},{8,16},{16,24},{1,9},{9,17},{17,25},{2,10},{10,18},{18,26},{... | collective-permute-start | bytes 3145736 | tf_op jit(solution)/shard_map/ppermute | solution.py:34
  78.9 1.4 collective-permute-start.5
  80.3 5.5 %collective-permute-start.4 = (f32[2,64,2048]{2,1,0:T(8,128)}, f32[2,64,2048]{2,1,0:T(8,128)}, u32[]{:S(2)}, u32[]{:S(2)}) collective-permute-start(f32[2,64,2048]{2,1,0:T(8,128)} %get-tuple-element.17), channel_id=1, source_target_pairs={{0,8},{8,16},{16,24},{1,9},{9,17},{17,25},{2,10},{10,18},{18,26},{... | collective-permute-start | bytes 3145736 | tf_op jit(solution)/shard_map/ppermute | solution.py:34
  85.8 1.3 collective-permute-start.7
  87.1 14.7 %collective-permute-done.6 = f32[2,64,2048]{2,1,0:T(8,128)} collective-permute-done((f32[2,64,2048]{2,1,0:T(8,128)}, f32[2,64,2048]{2,1,0:T(8,128)}, u32[]{:S(2)}, u32[]{:S(2)}) %collective-permute-start.6) | collective-permute-done | bytes 1048608 | tf_op jit(solution)/shard_map/ppermute | solution.py:34
  101.8 1.3 bitcast_dynamic-update-slice_fusion.20
  103.1 1.3 bitcast_dynamic-update-slice_fusion.19
  104.4 1.3 bitcast_dynamic-update-slice_fusion.18
  106.0 20.4 %collective-permute-done.7 = f32[2,64,2048]{2,1,0:T(8,128)S(1)} collective-permute-done((f32[2,64,2048]{2,1,0:T(8,128)}, f32[2,64,2048]{2,1,0:T(8,128)S(1)}, u32[]{:S(2)}, u32[]{:S(2)}) %collective-permute-start.7) | collective-permute-done | bytes 1048608 | tf_op jit(solution)/shard_map/ppermute | solution.py:35
  126.8 32.2 %fusion.2 = f32[512,4096]{1,0:T(8,128)} fusion(f32[512,2048]{1,0:T(8,128)S(1)} %bitcast.68, f32[4096,2048]{1,0:T(8,128)} %param.4), kind=kOutput, calls=%fused_computation.32 | convolution fusion | flops 25769803776 | bytes 46137344 | tf_op jit(solution)/shard_map/dot_general | solution.py:19
  159.1 2.3 collective-permute-start.8
  161.3 1.3 collective-permute-start.9
  162.6 18.2 %collective-permute-done.8 = f32[2,64,2048]{2,1,0:T(8,128)S(1)} collective-permute-done((f32[2,64,2048]{2,1,0:T(8,128)}, f32[2,64,2048]{2,1,0:T(8,128)S(1)}, u32[]{:S(2)}, u32[]{:S(2)}) %collective-permute-start.8) | collective-permute-done | bytes 1048608 | tf_op jit(solution)/shard_map/ppermute | solution.py:34
  180.8 4.1 collective-permute-done.9
  184.9 3.5 collective-permute-start.12
  188.4 1.5 collective-permute-start.11
  189.9 5.5 %collective-permute-start.10 = (f32[2,64,2048]{2,1,0:T(8,128)S(1)}, f32[2,64,2048]{2,1,0:T(8,128)}, u32[]{:S(2)}, u32[]{:S(2)}) collective-permute-start(f32[2,64,2048]{2,1,0:T(8,128)S(1)} %copy-done), channel_id=1, source_target_pairs={{0,8},{8,16},{16,24},{1,9},{9,17},{17,25},{2,10},{10,18},{18,26},{... | collective-permute-start | bytes 3145736 | tf_op jit(solution)/shard_map/ppermute | solution.py:34
  195.5 1.3 collective-permute-start.13
  196.8 15.2 %collective-permute-done.12 = f32[2,64,2048]{2,1,0:T(8,128)S(1)} collective-permute-done((f32[2,64,2048]{2,1,0:T(8,128)S(1)}, f32[2,64,2048]{2,1,0:T(8,128)S(1)}, u32[]{:S(2)}, u32[]{:S(2)}) %collective-permute-start.12) | collective-permute-done | bytes 1048608 | tf_op jit(solution)/shard_map/ppermute | solution.py:34
  212.1 1.3 bitcast_dynamic-update-slice_fusion.11
  213.5 1.5 bitcast_dynamic-update-slice_fusion.9
  215.2 17.9 %collective-permute-done.13 = f32[2,64,2048]{2,1,0:T(8,128)S(1)} collective-permute-done((f32[2,64,2048]{2,1,0:T(8,128)S(1)}, f32[2,64,2048]{2,1,0:T(8,128)S(1)}, u32[]{:S(2)}, u32[]{:S(2)}) %collective-permute-start.13) | collective-permute-done | bytes 1048608 | tf_op jit(solution)/shard_map/ppermute | solution.py:35
  233.4 32.2 %fusion.3 = f32[512,4096]{1,0:T(8,128)} fusion(f32[512,2048]{1,0:T(8,128)S(1)} %bitcast.69, f32[4096,2048]{1,0:T(8,128)} %param.4), kind=kOutput, calls=%fused_computation.33 | convolution fusion | flops 25769803776 | bytes 46137344 | tf_op jit(solution)/shard_map/dot_general | solution.py:19
  265.7 2.5 collective-permute-start.14
  268.1 1.3 collective-permute-start.16
  269.4 17.9 %collective-permute-done.14 = f32[2,64,2048]{2,1,0:T(8,128)S(1)} collective-permute-done((f32[2,64,2048]{2,1,0:T(8,128)}, f32[2,64,2048]{2,1,0:T(8,128)S(1)}, u32[]{:S(2)}, u32[]{:S(2)}) %collective-permute-start.14) | collective-permute-done | bytes 1048608 | tf_op jit(solution)/shard_map/ppermute | solution.py:34
  287.3 4.3 %collective-permute-start.15 = (f32[2,64,2048]{2,1,0:T(8,128)S(1)}, f32[2,64,2048]{2,1,0:T(8,128)S(1)}, u32[]{:S(2)}, u32[]{:S(2)}) collective-permute-start(f32[2,64,2048]{2,1,0:T(8,128)S(1)} %collective-permute-done.14), channel_id=1, source_target_pairs={{0,8},{8,16},{16,24},{1,9},{9,17},{17,25},{2,10},{10,18},{18,26},{... | collective-permute-start | bytes 3145736 | tf_op jit(solution)/shard_map/ppermute | solution.py:34
  291.7 1.5 collective-permute-start.17
  293.2 14.9 %collective-permute-done.15 = f32[2,64,2048]{2,1,0:T(8,128)S(1)} collective-permute-done((f32[2,64,2048]{2,1,0:T(8,128)S(1)}, f32[2,64,2048]{2,1,0:T(8,128)S(1)}, u32[]{:S(2)}, u32[]{:S(2)}) %collective-permute-start.15) | collective-permute-done | bytes 1048608 | tf_op jit(solution)/shard_map/ppermute | solution.py:34
  308.2 1.3 bitcast_dynamic-update-slice_fusion.4
  309.8 2.2 collective-permute-done.17
  312.4 32.3 %fusion.4 = f32[512,4096]{1,0:T(8,128)} fusion(f32[512,2048]{1,0:T(8,128)S(1)} %bitcast.67, f32[4096,2048]{1,0:T(8,128)} %param.4), kind=kOutput, calls=%fused_computation.34 | convolution fusion | flops 25769803776 | bytes 46137344 | tf_op jit(solution)/shard_map/dot_general | solution.py:19
  345.1 0.5 copy.6
  345.6 68.7 %reduce-scatter.8.cloned.1.call-done = f32[64,4096]{1,0:T(8,128)} async-done(((f32[512,4096]{1,0:T(8,128)}), f32[64,4096]{1,0:T(8,128)}) %reduce-scatter.8.cloned.1.call-update) | async-done | bytes 1048592 | tf_op jit(solution)/shard_map/reduce_scatter | solution.py:71
  414.4 4.0 fusion
  (49 shorter events, 3.3 us)
Async XLA Ops:
  6.5 339.1 %reduce-scatter.4.cloned.1.call-start = ((), (), s32[]{:S(2)}) async-start(), calls=%async_computation.3 | async-start | bytes 9437184 | tf_op jit(solution)/shard_map/reduce_scatter | solution.py:71
  16.9 28.1 %collective-permute-start.2 = (f32[2,64,2048]{2,1,0:T(8,128)S(1)}, f32[2,64,2048]{2,1,0:T(8,128)S(1)}, u32[]{:S(2)}, u32[]{:S(2)}) collective-permute-start(f32[2,64,2048]{2,1,0:T(8,128)S(1)} %get-tuple-element.31), channel_id=1, source_target_pairs={{8,0},{16,8},{24,16},{9,1},{17,9},{25,17},{10,2},{18,10},{26,18},{... | collective-permute-start | bytes 3145736 | tf_op jit(solution)/shard_map/ppermute | solution.py:35
  18.2 29.1 %collective-permute-start = (f32[2,64,2048]{2,1,0:T(8,128)S(1)}, f32[2,64,2048]{2,1,0:T(8,128)S(1)}, u32[]{:S(2)}, u32[]{:S(2)}) collective-permute-start(f32[2,64,2048]{2,1,0:T(8,128)S(1)} %get-tuple-element.31), channel_id=1, source_target_pairs={{0,8},{8,16},{16,24},{1,9},{9,17},{17,25},{2,10},{10,18},{18,26},{... | collective-permute-start | bytes 3145736 | tf_op jit(solution)/shard_map/ppermute | solution.py:34
  45.0 1.0 copy-start.2
  46.0 26.2 %collective-permute-start.3 = (f32[2,64,2048]{2,1,0:T(8,128)S(1)}, f32[2,64,2048]{2,1,0:T(8,128)S(1)}, u32[]{:S(2)}, u32[]{:S(2)}) collective-permute-start(f32[2,64,2048]{2,1,0:T(8,128)S(1)} %collective-permute-done.2), channel_id=1, source_target_pairs={{8,0},{16,8},{24,16},{9,1},{17,9},{25,17},{10,2},{18,10},{26,18},{... | collective-permute-start | bytes 3145736 | tf_op jit(solution)/shard_map/ppermute | solution.py:35
  47.3 26.1 %copy-start.6 = (f32[2,64,2048]{2,1,0:T(8,128)}, f32[2,64,2048]{2,1,0:T(8,128)S(1)}, u32[]{:S(2)}) copy-start(f32[2,64,2048]{2,1,0:T(8,128)S(1)} %collective-permute-done) | copy-start | bytes 3145732
  47.3 26.1 %collective-permute-start.1 = (f32[2,64,2048]{2,1,0:T(8,128)S(1)}, f32[2,64,2048]{2,1,0:T(8,128)}, u32[]{:S(2)}, u32[]{:S(2)}) collective-permute-start(f32[2,64,2048]{2,1,0:T(8,128)S(1)} %collective-permute-done), channel_id=1, source_target_pairs={{0,8},{8,16},{16,24},{1,9},{9,17},{17,25},{2,10},{10,18},{18,26},{... | collective-permute-start | bytes 3145736 | tf_op jit(solution)/shard_map/ppermute | solution.py:34
  72.2 1.0 copy-start.4
  73.4 28.4 %collective-permute-start.6 = (f32[2,64,2048]{2,1,0:T(8,128)}, f32[2,64,2048]{2,1,0:T(8,128)}, u32[]{:S(2)}, u32[]{:S(2)}) collective-permute-start(f32[2,64,2048]{2,1,0:T(8,128)} %collective-permute-done.1), channel_id=1, source_target_pairs={{0,8},{8,16},{16,24},{1,9},{9,17},{17,25},{2,10},{10,18},{18,26},{... | collective-permute-start | bytes 3145736 | tf_op jit(solution)/shard_map/ppermute | solution.py:34
  78.9 26.9 %copy-start.3 = (f32[2,64,2048]{2,1,0:T(8,128)S(1)}, f32[2,64,2048]{2,1,0:T(8,128)}, u32[]{:S(2)}) copy-start(f32[2,64,2048]{2,1,0:T(8,128)} %copy-done.2) | copy-start | bytes 3145732
  78.9 27.0 %copy-start.5 = (f32[2,64,2048]{2,1,0:T(8,128)S(1)}, f32[2,64,2048]{2,1,0:T(8,128)}, u32[]{:S(2)}) copy-start(f32[2,64,2048]{2,1,0:T(8,128)} %copy-done.4) | copy-start | bytes 3145732
  78.9 80.1 %collective-permute-start.5 = (f32[2,64,2048]{2,1,0:T(8,128)}, f32[2,64,2048]{2,1,0:T(8,128)}, u32[]{:S(2)}, u32[]{:S(2)}) collective-permute-start(f32[2,64,2048]{2,1,0:T(8,128)} %get-tuple-element.17), channel_id=1, source_target_pairs={{8,0},{16,8},{24,16},{9,1},{17,9},{25,17},{10,2},{18,10},{26,18},{... | collective-permute-start | bytes 3145736 | tf_op jit(solution)/shard_map/ppermute | solution.py:35
  80.3 78.7 %collective-permute-start.4 = (f32[2,64,2048]{2,1,0:T(8,128)}, f32[2,64,2048]{2,1,0:T(8,128)}, u32[]{:S(2)}, u32[]{:S(2)}) collective-permute-start(f32[2,64,2048]{2,1,0:T(8,128)} %get-tuple-element.17), channel_id=1, source_target_pairs={{0,8},{8,16},{16,24},{1,9},{9,17},{17,25},{2,10},{10,18},{18,26},{... | collective-permute-start | bytes 3145736 | tf_op jit(solution)/shard_map/ppermute | solution.py:34
  85.8 40.6 %collective-permute-start.7 = (f32[2,64,2048]{2,1,0:T(8,128)}, f32[2,64,2048]{2,1,0:T(8,128)S(1)}, u32[]{:S(2)}, u32[]{:S(2)}) collective-permute-start(f32[2,64,2048]{2,1,0:T(8,128)} %copy-done.4), channel_id=1, source_target_pairs={{8,0},{16,8},{24,16},{9,1},{17,9},{25,17},{10,2},{18,10},{26,18},{... | collective-permute-start | bytes 3145736 | tf_op jit(solution)/shard_map/ppermute | solution.py:35
  159.0 29.5 %copy-start = (f32[2,64,2048]{2,1,0:T(8,128)S(1)}, f32[2,64,2048]{2,1,0:T(8,128)}, u32[]{:S(2)}) copy-start(f32[2,64,2048]{2,1,0:T(8,128)} %get-tuple-element.23) | copy-start | bytes 3145732
  159.0 54.4 %copy-start.1 = (f32[2,64,2048]{2,1,0:T(8,128)S(1)}, f32[2,64,2048]{2,1,0:T(8,128)}, u32[]{:S(2)}) copy-start(f32[2,64,2048]{2,1,0:T(8,128)} %get-tuple-element.17) | copy-start | bytes 3145732
  159.0 186.6 %reduce-scatter.6.cloned.1.call-start = ((), (), s32[]{:S(2)}) async-start(), calls=%async_computation.4 | async-start | bytes 9437184 | tf_op jit(solution)/shard_map/reduce_scatter | solution.py:71
  159.1 21.7 %collective-permute-start.8 = (f32[2,64,2048]{2,1,0:T(8,128)}, f32[2,64,2048]{2,1,0:T(8,128)S(1)}, u32[]{:S(2)}, u32[]{:S(2)}) collective-permute-start(f32[2,64,2048]{2,1,0:T(8,128)} %collective-permute-done.4), channel_id=1, source_target_pairs={{0,8},{8,16},{16,24},{1,9},{9,17},{17,25},{2,10},{10,18},{18,26},{... | collective-permute-start | bytes 3145736 | tf_op jit(solution)/shard_map/ppermute | solution.py:34
  161.3 23.6 %collective-permute-start.9 = (f32[2,64,2048]{2,1,0:T(8,128)}, f32[2,64,2048]{2,1,0:T(8,128)S(1)}, u32[]{:S(2)}, u32[]{:S(2)}) collective-permute-start(f32[2,64,2048]{2,1,0:T(8,128)} %collective-permute-done.5), channel_id=1, source_target_pairs={{8,0},{16,8},{24,16},{9,1},{17,9},{25,17},{10,2},{18,10},{26,18},{... | collective-permute-start | bytes 3145736 | tf_op jit(solution)/shard_map/ppermute | solution.py:35
  184.9 27.1 %collective-permute-start.12 = (f32[2,64,2048]{2,1,0:T(8,128)S(1)}, f32[2,64,2048]{2,1,0:T(8,128)S(1)}, u32[]{:S(2)}, u32[]{:S(2)}) collective-permute-start(f32[2,64,2048]{2,1,0:T(8,128)S(1)} %collective-permute-done.8), channel_id=1, source_target_pairs={{0,8},{8,16},{16,24},{1,9},{9,17},{17,25},{2,10},{10,18},{18,26},{... | collective-permute-start | bytes 3145736 | tf_op jit(solution)/shard_map/ppermute | solution.py:34
  188.4 77.1 %collective-permute-start.11 = (f32[2,64,2048]{2,1,0:T(8,128)S(1)}, f32[2,64,2048]{2,1,0:T(8,128)S(1)}, u32[]{:S(2)}, u32[]{:S(2)}) collective-permute-start(f32[2,64,2048]{2,1,0:T(8,128)S(1)} %copy-done), channel_id=1, source_target_pairs={{8,0},{16,8},{24,16},{9,1},{17,9},{25,17},{10,2},{18,10},{26,18},{... | collective-permute-start | bytes 3145736 | tf_op jit(solution)/shard_map/ppermute | solution.py:35
  189.9 75.7 %collective-permute-start.10 = (f32[2,64,2048]{2,1,0:T(8,128)S(1)}, f32[2,64,2048]{2,1,0:T(8,128)}, u32[]{:S(2)}, u32[]{:S(2)}) collective-permute-start(f32[2,64,2048]{2,1,0:T(8,128)S(1)} %copy-done), channel_id=1, source_target_pairs={{0,8},{8,16},{16,24},{1,9},{9,17},{17,25},{2,10},{10,18},{18,26},{... | collective-permute-start | bytes 3145736 | tf_op jit(solution)/shard_map/ppermute | solution.py:34
  195.5 37.6 %collective-permute-start.13 = (f32[2,64,2048]{2,1,0:T(8,128)S(1)}, f32[2,64,2048]{2,1,0:T(8,128)S(1)}, u32[]{:S(2)}, u32[]{:S(2)}) collective-permute-start(f32[2,64,2048]{2,1,0:T(8,128)S(1)} %collective-permute-done.9), channel_id=1, source_target_pairs={{8,0},{16,8},{24,16},{9,1},{17,9},{25,17},{10,2},{18,10},{26,18},{... | collective-permute-start | bytes 3145736 | tf_op jit(solution)/shard_map/ppermute | solution.py:35
  265.6 148.7 %reduce-scatter.8.cloned.1.call-start = ((), (), s32[]{:S(2)}) async-start(), calls=%async_computation.5 | async-start | bytes 9437184 | tf_op jit(solution)/shard_map/reduce_scatter | solution.py:71
  265.7 21.7 %collective-permute-start.14 = (f32[2,64,2048]{2,1,0:T(8,128)}, f32[2,64,2048]{2,1,0:T(8,128)S(1)}, u32[]{:S(2)}, u32[]{:S(2)}) collective-permute-start(f32[2,64,2048]{2,1,0:T(8,128)} %collective-permute-done.10), channel_id=1, source_target_pairs={{0,8},{8,16},{16,24},{1,9},{9,17},{17,25},{2,10},{10,18},{18,26},{... | collective-permute-start | bytes 3145736 | tf_op jit(solution)/shard_map/ppermute | solution.py:34
  268.1 23.5 %collective-permute-start.16 = (f32[2,64,2048]{2,1,0:T(8,128)S(1)}, f32[2,64,2048]{2,1,0:T(8,128)S(1)}, u32[]{:S(2)}, u32[]{:S(2)}) collective-permute-start(f32[2,64,2048]{2,1,0:T(8,128)S(1)} %collective-permute-done.11), channel_id=1, source_target_pairs={{8,0},{16,8},{24,16},{9,1},{17,9},{25,17},{10,2},{18,10},{26,18},{... | collective-permute-start | bytes 3145736 | tf_op jit(solution)/shard_map/ppermute | solution.py:35
  287.3 20.7 %collective-permute-start.15 = (f32[2,64,2048]{2,1,0:T(8,128)S(1)}, f32[2,64,2048]{2,1,0:T(8,128)S(1)}, u32[]{:S(2)}, u32[]{:S(2)}) collective-permute-start(f32[2,64,2048]{2,1,0:T(8,128)S(1)} %collective-permute-done.14), channel_id=1, source_target_pairs={{0,8},{8,16},{16,24},{1,9},{9,17},{17,25},{2,10},{10,18},{18,26},{... | collective-permute-start | bytes 3145736 | tf_op jit(solution)/shard_map/ppermute | solution.py:34
  291.7 20.3 %collective-permute-start.17 = (f32[2,64,2048]{2,1,0:T(8,128)S(1)}, f32[2,64,2048]{2,1,0:T(8,128)S(1)}, u32[]{:S(2)}, u32[]{:S(2)}) collective-permute-start(f32[2,64,2048]{2,1,0:T(8,128)S(1)} %collective-permute-done.16), channel_id=1, source_target_pairs={{8,0},{16,8},{24,16},{9,1},{17,9},{25,17},{10,2},{18,10},{26,18},{... | collective-permute-start | bytes 3145736 | tf_op jit(solution)/shard_map/ppermute | solution.py:35
Sparse Core Ops, SparseCore 0:
  159.1 70.1 reduce-scatter.3
  265.7 69.4 reduce-scatter.5
  344.8 69.5 reduce-scatter.7
